TPU v7x, 32 devices: a whole 2x2x4 slice. The times are simulated.
32 devices in a mesh: dp: 4 (over y, core), wide: 4 (over z), narrow: 2 (over x).
Axes of the slice: x: 2, y: 2, z: 4, core: 2. Of those that a mesh axis runs over, the one named last changes fastest.
Arguments:
- patches: bfloat16 [2, 38535168], P('narrow', ('dp', 'wide')), may hold values from -6 to 6
- visible: int32 [512, 49], P(('dp', 'wide')), may hold values from 0 to 195, as said below
- w_qkv: bfloat16 [768, 3, 768], P('narrow', None, 'wide'), may hold values from -0.3125 to 0.3125
- b_qv: bfloat16 [2, 768], P(None, 'wide'), may hold values from -3 to 3
- w_out: bfloat16 [768, 768], P('wide', 'narrow'), may hold values from -0.875 to 0.875
- b_out: bfloat16 [768], P('narrow'), may hold values from -2 to 2
- w_up: bfloat16 [768, 3072], P('narrow', 'wide'), may hold values from -0.21875 to 0.21875
- b_up: bfloat16 [3072], P('wide'), may hold values from -3 to 3
- w_down: bfloat16 [768, 3072], P('narrow', 'wide'), may hold values from -0.15625 to 0.15625
- b_down: bfloat16 [768], P('narrow'), may hold values from -2 to 2
- gain_one: bfloat16 [768], P('narrow'), may hold values from 0.099609375 to 1.8984375
- shift_one: bfloat16 [768], P('narrow'), may hold values from -2 to 2
- gain_two: bfloat16 [768], P('narrow'), may hold values from 0.099609375 to 1.8984375
- shift_two: bfloat16 [768], P('narrow'), may hold values from -2 to 2
- cotangent: bfloat16 [2, 9633792], P('narrow', ('dp', 'wide')), may hold values from -6 to 6
Outputs:
- block_output: bfloat16 [2, 9633792], P('narrow', ('dp', 'wide'))
- grad_patches: float32 [2, 38535168], P('narrow', ('dp', 'wide'))
- grad_wqkv: float32 [768, 3, 768], P('narrow', None, 'wide')
- grad_bqv: float32 [2, 768], P(None, 'wide')
- grad_wout: float32 [768, 768], P('wide', 'narrow')
- grad_bout: float32 [768], P('narrow')
- grad_wup: float32 [768, 3072], P('narrow', 'wide')
- grad_bup: float32 [3072], P('wide')
- grad_wdown: float32 [768, 3072], P('narrow', 'wide')
- grad_bdown: float32 [768], P('narrow')
- grad_gain1: float32 [768], P('narrow')
- grad_shift1: float32 [768], P('narrow')
- grad_gain2: float32 [768], P('narrow')
- grad_shift2: float32 [768], P('narrow')
Inputs may be any that keep to these rules, and one draw needn't show every extreme that they name: `visible`: each image's 49 indices are distinct and increasing.
All inputs are finite; a program needn't handle non-finite values.
Results may differ from a plain program's by a relative error of at most 0.012.
The roundings to bfloat16 on the way count: a program that leaves them out, or rounds other values in their place, can miss the bound.
Values may be sent and summed in bfloat16 or wider, within the bound.
No kernel may reach another device: no remote copies, remote signals or barrier semaphores. Data moves between devices by JAX's collectives and lax.ppermute only.
A program may use at most 256 MiB of HBM per device.

v0:
```python
from functools import partial
import jax
import jax.numpy as jnp
from jax import lax
from jax.sharding import PartitionSpec as P

D = 768
HEAD_DIM = 64
PATCHES = 196
VISIBLE = 49
epsilon = 1e-06


def narrow_product(acts, weight):
    return lax.psum_scatter(
        jnp.dot(acts, weight, preferred_element_type=jnp.float32),
        "narrow",
        scatter_dimension=0,
        tiled=True,
    )


def normalize(values, gain, shift):
    totals = lax.psum((jnp.sum(values, 1), jnp.sum(values * values, 1)), "narrow")
    row_mean = totals[0] / D
    row_var = totals[1] / D - row_mean * row_mean
    inv_std = lax.rsqrt(row_var + epsilon)
    normed = (values - row_mean[:, None]) * inv_std[:, None]
    return (normed, inv_std, (normed * gain + shift).astype(jnp.bfloat16))


def norm_back(grad, normed, inv_std, gain):
    scaled = grad * gain
    totals = lax.psum((jnp.sum(scaled, 1), jnp.sum(scaled * normed, 1)), "narrow")
    back = inv_std[:, None] * (scaled - totals[0][:, None] / D - normed * (totals[1][:, None] / D))
    return (back, jnp.sum(grad * normed, 0), jnp.sum(grad, 0))


def wide_rows(acts):
    return lax.all_gather(acts, "wide", axis=0, tiled=True)


def narrow_rows(acts):
    return lax.all_gather(acts, "narrow", axis=0, tiled=True)


def wide_sum(partial_rows):
    return lax.psum_scatter(partial_rows, "wide", scatter_dimension=0, tiled=True)


def grad_wide_rows(acts):
    return lax.all_gather(acts, "wide", axis=0, tiled=True)


def grad_narrow_rows(acts):
    return lax.all_gather(acts, "narrow", axis=0, tiled=True)


def grad_wide_sum(partial_rows):
    return lax.psum_scatter(partial_rows, "wide", scatter_dimension=0, tiled=True)


def outer_sum(left, right):
    return lax.dot_general(
        left, right, (((0,), (0,)), ((), ())), preferred_element_type=jnp.float32
    )


def times_trans(left, weight):
    return lax.dot_general(
        left, weight, (((1,), (1,)), ((), ())), preferred_element_type=jnp.float32
    )


def attend(queries, keys_all, values_all, scale):
    scores = (
        jnp.einsum("nqhd,nkhd->nhqk", queries, keys_all, preferred_element_type=jnp.float32) * scale
    )
    top_score = jnp.max(scores, -1, keepdims=True)
    expo = jnp.exp(scores - top_score)
    total = jnp.sum(expo, -1, keepdims=True)
    prob_low = (expo / total).astype(jnp.bfloat16)
    mixed = jnp.einsum("nhqk,nkhd->nqhd", prob_low, values_all, preferred_element_type=jnp.float32)
    return (mixed, top_score + jnp.log(total))


def attend_back(queries, keys_all, values_all, log_total, grad_mixed, scale):
    scores = (
        jnp.einsum("nqhd,nkhd->nhqk", queries, keys_all, preferred_element_type=jnp.float32) * scale
    )
    attn_prob = jnp.exp(scores - log_total)
    grad_values = jnp.einsum(
        "nhqk,nqhd->nkhd",
        attn_prob.astype(jnp.bfloat16),
        grad_mixed,
        preferred_element_type=jnp.float32,
    )
    grad_prob = jnp.einsum(
        "nqhd,nkhd->nhqk", grad_mixed, values_all, preferred_element_type=jnp.float32
    )
    grad_scores = attn_prob * (grad_prob - jnp.sum(grad_prob * attn_prob, -1, keepdims=True))
    grad_scores = grad_scores.astype(jnp.bfloat16)
    grad_queries = (
        jnp.einsum("nhqk,nkhd->nqhd", grad_scores, keys_all, preferred_element_type=jnp.float32)
        * scale
    )
    grad_keys = (
        jnp.einsum("nhqk,nqhd->nkhd", grad_scores, queries, preferred_element_type=jnp.float32)
        * scale
    )
    return (grad_queries, grad_keys, grad_values)


def on_device(
    patches,
    visible,
    w_qkv,
    b_qv,
    w_out,
    b_out,
    w_up,
    b_up,
    w_down,
    b_down,
    gain_one,
    shift_one,
    gain_two,
    shift_two,
    cotangent,
):
    local_images = visible.shape[0]
    narrow_cols = w_qkv.shape[0]
    patch_rows = patches.reshape(local_images, PATCHES, narrow_cols)
    qkv_use, bqv_use, wout_use, wup_use, bup_use, wdown_use = (
        w_qkv,
        b_qv,
        w_out,
        w_up,
        b_up,
        w_down,
    )
    wide_cols = qkv_use.shape[2]
    head_count = wide_cols // HEAD_DIM
    scale = HEAD_DIM ** (-0.5)
    gain_a = gain_one.astype(jnp.float32)
    gain_b = gain_two.astype(jnp.float32)
    w_qkv_flat = qkv_use.reshape(narrow_cols, 3 * wide_cols)
    vis_rows = (
        jnp.take_along_axis(patch_rows, visible[:, :, None], axis=1)
        .reshape(-1, narrow_cols)
        .astype(jnp.float32)
    )
    normed_one, inv_one, hidden_one = normalize(vis_rows, gain_a, shift_one.astype(jnp.float32))
    hidden_one_all = wide_rows(hidden_one)
    bias_row = jnp.concatenate(
        [
            bqv_use[0].astype(jnp.float32),
            jnp.zeros((wide_cols,), jnp.float32),
            bqv_use[1].astype(jnp.float32),
        ]
    )
    triple = (narrow_product(hidden_one_all, w_qkv_flat) + bias_row).astype(jnp.bfloat16)
    image_count = triple.shape[0] // VISIBLE
    split = triple.reshape(image_count, VISIBLE, 3, head_count, HEAD_DIM)
    queries = split[:, :, 0]
    keys_all = split[:, :, 1]
    values_all = split[:, :, 2]
    mixed, log_total = attend(queries, keys_all, values_all, scale)
    mixed = mixed.reshape(-1, wide_cols).astype(jnp.bfloat16)
    mixed_all = narrow_rows(mixed)
    middle = vis_rows + (
        wide_sum(jnp.dot(mixed_all, wout_use, preferred_element_type=jnp.float32))
        + b_out.astype(jnp.float32)
    )
    normed_two, inv_two, hidden_two = normalize(middle, gain_b, shift_two.astype(jnp.float32))
    hidden_two_all = wide_rows(hidden_two)
    inner = narrow_product(hidden_two_all, wup_use) + bup_use.astype(jnp.float32)
    gelu_exact = partial(jax.nn.gelu, approximate=False)
    active = gelu_exact(inner).astype(jnp.bfloat16)
    active_all = narrow_rows(active)
    result = middle + (wide_sum(times_trans(active_all, wdown_use)) + b_down.astype(jnp.float32))
    block_output = result.astype(jnp.bfloat16).reshape(1, -1)
    cot_rows = cotangent.reshape(-1, narrow_cols)
    grad_out = cot_rows.astype(jnp.float32)
    grad_down_all = grad_wide_rows(cot_rows)
    gw_down = outer_sum(grad_down_all, active_all)
    gb_down = jnp.sum(grad_down_all, 0, dtype=jnp.float32)
    grad_active = narrow_product(grad_down_all, wdown_use)
    gelu_pull = jax.vjp(gelu_exact, inner)[1]
    grad_inner = gelu_pull(grad_active)[0].astype(jnp.bfloat16)
    grad_inner_all = grad_narrow_rows(grad_inner)
    gw_up = outer_sum(hidden_two_all, grad_inner_all)
    gb_up = jnp.sum(grad_inner_all, 0, dtype=jnp.float32)
    grad_hidden_two = grad_wide_sum(times_trans(grad_inner_all, wup_use))
    back_two, gg_two, gs_two = norm_back(grad_hidden_two, normed_two, inv_two, gain_b)
    grad_middle = grad_out + back_two
    grad_branch_all = grad_wide_rows(grad_middle.astype(jnp.bfloat16))
    gw_out = outer_sum(mixed_all, grad_branch_all)
    gb_out = jnp.sum(grad_branch_all, 0, dtype=jnp.float32)
    grad_mixed = narrow_product(grad_branch_all, wout_use.T).astype(jnp.bfloat16)
    grad_mixed = grad_mixed.reshape(image_count, VISIBLE, head_count, HEAD_DIM)
    grad_queries, grad_keys, grad_values = attend_back(
        queries, keys_all, values_all, log_total, grad_mixed, scale
    )
    grad_triple = (
        jnp.stack([grad_queries, grad_keys, grad_values], 2)
        .reshape(-1, 3 * wide_cols)
        .astype(jnp.bfloat16)
    )
    grad_triple_all = grad_narrow_rows(grad_triple)
    gw_qkv = outer_sum(hidden_one_all, grad_triple_all).reshape(narrow_cols, 3, wide_cols)
    bias_sums = jnp.sum(grad_triple_all, 0, dtype=jnp.float32).reshape(3, wide_cols)
    gb_qv = jnp.stack([bias_sums[0], bias_sums[2]])
    grad_hidden_one = grad_wide_sum(times_trans(grad_triple_all, w_qkv_flat))
    back_one, gg_one, gs_one = norm_back(grad_hidden_one, normed_one, inv_one, gain_a)
    grad_rows = grad_middle + back_one
    image_index = jnp.arange(local_images)[:, None]
    grad_patches = (
        jnp.zeros((local_images, PATCHES, narrow_cols), jnp.float32)
        .at[image_index, visible]
        .set(grad_rows.reshape(local_images, VISIBLE, narrow_cols))
    )
    grad_patches = grad_patches.reshape(1, -1)
    summed = lax.psum((gw_qkv, gb_qv, gw_out, gb_out, gw_up, gb_up, gw_down, gb_down), "dp")
    vectors = lax.psum((gg_one, gs_one, gg_two, gs_two), ("dp", "wide"))
    return (
        block_output,
        grad_patches,
        summed[0],
        summed[1],
        summed[2],
        summed[3],
        summed[4],
        summed[5],
        summed[6],
        summed[7],
        vectors[0],
        vectors[1],
        vectors[2],
        vectors[3],
    )


def solution(mesh):
    in_specs = (
        P("narrow", ("dp", "wide")),
        P(("dp", "wide"), None),
        P("narrow", None, "wide"),
        P(None, "wide"),
        P("wide", "narrow"),
        P("narrow"),
        P("narrow", "wide"),
        P("wide"),
        P("narrow", "wide"),
        P("narrow"),
        P("narrow"),
        P("narrow"),
        P("narrow"),
        P("narrow"),
        P("narrow", ("dp", "wide")),
    )
    out_specs = (
        P("narrow", ("dp", "wide")),
        P("narrow", ("dp", "wide")),
        P("narrow", None, "wide"),
        P(None, "wide"),
        P("wide", "narrow"),
        P("narrow"),
        P("narrow", "wide"),
        P("wide"),
        P("narrow", "wide"),
        P("narrow"),
        P("narrow"),
        P("narrow"),
        P("narrow"),
        P("narrow"),
    )
    return jax.shard_map(
        on_device, mesh=mesh, in_specs=in_specs, out_specs=out_specs, check_vma=False
    )
```

profile of v0, /device:TPU:0, one launch (start us, length us, event | category | flops | bytes accessed | tf_op | source)
XLA Modules:
  0.0 2732.8 jit_solution(15280021996956817729)
XLA Ops:
  10.3 103.4 %reduce.4 = bf16[2408448]{0:T(1024)(128)(2,1)} reduce(bf16[1,2408448]{1,0:T(2,128)(2,1)} %param.15, bf16[]{:T(256)} %constant.125), dimensions={0}, to_apply=%param.15.reduce_sub_computation | reduce | bytes 9633794 | tf_op args[0]
  126.9 22.3 gather_fusion
  163.7 91.1 %all-gather.11.cloned.1.call-done = bf16[6272,384]{1,0:T(8,128)(2,1)} async-done(((bf16[1568,384]{1,0:T(8,128)(2,1)}), bf16[6272,384]{1,0:T(8,128)(2,1)}) %all-gather.11.cloned.1.call-update) | async-done | bytes 4816912 | tf_op jit(solution)/shard_map/all_gather | solution.py:40
  265.5 179.2 %reduce-scatter.25.cloned.1.call-done = f32[3136,576]{1,0:T(8,128)} async-done(((f32[6272,576]{1,0:T(8,128)}), f32[3136,576]{1,0:T(8,128)}) %reduce-scatter.25.cloned.1.call-update) | async-done | bytes 7225360
  459.3 29.2 %reshape.125 = bf16[64,49,3,3,64]{1,0,4,3,2:T(8,128)(2,1)} reshape(bf16[3136,576]{0,1:T(8,128)(2,1)} %add_convert_fusion.1) | data formatting | bytes 7225344 | tf_op jit(solution)/shard_map/reshape | solution.py:164
  530.0 14.5 reshape.152
  544.6 37.3 %all-gather.23.cloned.1.call-done = bf16[2,3136,192]{1,2,0:T(8,128)(2,1)} async-done(((bf16[1,3136,192]{1,2,0:T(8,128)(2,1)}), bf16[2,3136,192]{1,2,0:T(8,128)(2,1)}) %all-gather.23.cloned.1.call-update) | async-done | bytes 2408464 | tf_op jit(solution)/shard_map/all_gather | solution.py:44
  599.8 26.0 reduce.5
  627.4 136.9 %reduce-scatter.13.cloned.1.call-done = f32[1568,384]{1,0:T(8,128)} async-done(((f32[6272,384]{1,0:T(8,128)}), f32[1568,384]{1,0:T(8,128)}) %reduce-scatter.13.cloned.1.call-update) | async-done | bytes 2408464 | tf_op jit(solution)/shard_map/reduce_scatter | solution.py:48
  779.7 77.9 %all-gather.17.cloned.1.call-done = bf16[6272,384]{1,0:T(8,128)(2,1)} async-done(((bf16[1568,384]{1,0:T(8,128)(2,1)}), bf16[6272,384]{1,0:T(8,128)(2,1)}) %all-gather.17.cloned.1.call-update) | async-done | bytes 4816912 | tf_op jit(solution)/shard_map/all_gather | solution.py:52
  869.2 79.9 %all-gather.13.cloned.1.call-done = bf16[6272,384]{1,0:T(8,128)(2,1)} async-done(((bf16[1568,384]{1,0:T(8,128)(2,1)}), bf16[6272,384]{1,0:T(8,128)(2,1)}) %all-gather.13.cloned.1.call-update) | async-done | bytes 4816912 | tf_op jit(solution)/shard_map/all_gather | solution.py:40
  961.3 204.5 %reduce-scatter.19.cloned.1.call-done = f32[3136,768]{1,0:T(8,128)} async-done(((f32[6272,768]{1,0:T(8,128)}), f32[3136,768]{1,0:T(8,128)}) %reduce-scatter.19.cloned.1.call-update) | async-done | bytes 9633808 | tf_op jit(solution)/shard_map/reduce_scatter | solution.py:15
  1165.8 218.2 %reduce-scatter.15.cloned.1.call-done = f32[3136,768]{1,0:T(8,128)} async-done(((f32[6272,768]{1,0:T(8,128)}), f32[3136,768]{1,0:T(8,128)}) %reduce-scatter.15.cloned.1.call-update) | async-done | bytes 9633808 | tf_op jit(solution)/shard_map/reduce_scatter | solution.py:15
  1384.0 25.5 add_convert_fusion
  1420.7 109.2 %all-gather.19.cloned.1.call-done = bf16[6272,768]{1,0:T(8,128)(2,1)} async-done(((bf16[3136,768]{1,0:T(8,128)(2,1)}), bf16[6272,768]{1,0:T(8,128)(2,1)}) %all-gather.19.cloned.1.call-update) | async-done | bytes 9633808 | tf_op jit(solution)/shard_map/all_gather | solution.py:56
  1541.5 110.0 %all-gather.15.cloned.1.call-done = bf16[6272,768]{1,0:T(8,128)(2,1)} async-done(((bf16[3136,768]{1,0:T(8,128)(2,1)}), bf16[6272,768]{1,0:T(8,128)(2,1)}) %all-gather.15.cloned.1.call-update) | async-done | bytes 9633808 | tf_op jit(solution)/shard_map/all_gather | solution.py:44
  1663.1 155.7 %reduce-scatter.21.cloned.1.call-done = f32[1568,384]{1,0:T(8,128)} async-done(((f32[6272,384]{1,0:T(8,128)}), f32[1568,384]{1,0:T(8,128)}) %reduce-scatter.21.cloned.1.call-update) | async-done | bytes 2408464 | tf_op jit(solution)/shard_map/reduce_scatter | solution.py:60
  1829.8 156.6 %reduce-scatter.17.cloned.1.call-done = f32[1568,384]{1,0:T(8,128)} async-done(((f32[6272,384]{1,0:T(8,128)}), f32[1568,384]{1,0:T(8,128)}) %reduce-scatter.17.cloned.1.call-update) | async-done | bytes 2408464 | tf_op jit(solution)/shard_map/reduce_scatter | solution.py:48
  1991.3 92.0 %all-gather.21.cloned.1.call-done = bf16[6272,384]{1,0:T(8,128)(2,1)} async-done(((bf16[1568,384]{1,0:T(8,128)(2,1)}), bf16[6272,384]{1,0:T(8,128)(2,1)}) %all-gather.21.cloned.1.call-update) | async-done | bytes 4816912 | tf_op jit(solution)/shard_map/all_gather | solution.py:52
  2090.6 76.8 %reduce-scatter.27.cloned.1.call-done = f32[3136,192]{1,0:T(8,128)} async-done(((f32[6272,192]{1,0:T(8,128)}), f32[3136,192]{1,0:T(8,128)}) %reduce-scatter.27.cloned.1.call-update) | async-done | bytes 2408464
  2204.5 13.5 copy.73
  2218.0 15.0 reshape.154
  2257.6 68.1 %all-gather.25.cloned.1.call-done = bf16[2,3136,576]{1,2,0:T(8,128)(2,1)} async-done(((bf16[1,3136,576]{1,2,0:T(8,128)(2,1)}), bf16[2,3136,576]{1,2,0:T(8,128)(2,1)}) %all-gather.25.cloned.1.call-update) | async-done | bytes 7225360 | tf_op jit(solution)/shard_map/all_gather | solution.py:56
  2325.7 39.5 %copy.74 = bf16[2,3136,576]{1,0,2:T(2,128)(2,1)} copy(bf16[2,3136,576]{1,2,0:T(8,128)(2,1)} %all-gather.25.cloned.1.call-done) | data formatting | bytes 14450688 | tf_op jit(solution)/shard_map/all_gather | solution.py:56
  2365.3 11.8 reshape.155
  2420.4 11.7 all-reduce.1
  2432.2 29.8 %all-reduce.9.cloned.1.call-done = (f32[384,3,192]{0,2,1:T(8,128)}, f32[192,384]{1,0:T(8,128)}, f32[384,768]{1,0:T(8,128)}, f32[384,768]{0,1:T(8,128)}) async-done(((f32[384,3,192]{0,2,1:T(8,128)}, f32[192,384]{1,0:T(8,128)}, f32[384,768]{1,0:T(8,128)}, f32[384,768]{0,1:T(8,128)}), (f32[384,3,192]{0,2,1:T(8,128)}, f32[192,384]{1,0:T(8,128)}, f32[384,768]{1,0:T(8,128)}, ...) | async-done | bytes 3538960 | tf_op jit(solution)/shard_map/psum | solution.py:224
  2464.6 164.8 %reduce-scatter.23.cloned.1.call-done = f32[1568,384]{1,0:T(8,128)} async-done(((f32[6272,384]{1,0:T(8,128)}), f32[1568,384]{1,0:T(8,128)}) %reduce-scatter.23.cloned.1.call-update) | async-done | bytes 2408464 | tf_op jit(solution)/shard_map/reduce_scatter | solution.py:60
  2640.5 18.2 scatter_custom_fusion
  2658.7 13.1 copy.75
  2671.8 18.9 reshape.130
  2690.7 32.5 %all-reduce = (f32[384]{0:T(512)}, f32[384]{0:T(512)}, f32[384]{0:T(512)}, f32[384]{0:T(512)}) all-reduce(f32[384]{0:T(512)S(1)} %get-tuple-element.72, f32[384]{0:T(512)S(1)} %get-tuple-element.77, f32[384]{0:T(512)S(1)} %get-tuple-element.70, f32[384]{0:T(512)S(1)} %get-tuple-element.76), channel_id=1, replica_groups=mesh['dp'=4,'wide'=4,'narrow'=2] {'dp','wide'}, use_global_device_ids=true, to_apply=%region_41.42 | all-reduce | flops 1536 | bytes 12288 | tf_op jit(solution)/shard_map/psum | solution.py:225
  (216 shorter events, 334.5 us)
Async XLA Ops:
  7.2 941.9 %copy-start = (bf16[384,768]{1,0:T(8,128)(2,1)S(1)}, bf16[384,768]{1,0:T(8,128)(2,1)}, u32[]{:S(2)}) copy-start(bf16[384,768]{1,0:T(8,128)(2,1)} %param.21) | copy-start | bytes 1769476
  7.2 247.6 %all-gather.11.cloned.1.call-start = ((), (), s32[]{:S(2)}) async-start(), calls=%async_computation.8 | async-start | bytes 6021120 | tf_op jit(solution)/shard_map/all_gather | solution.py:40
  9.4 151.3 %copy-start.27 = (f32[384]{0:T(512)}, f32[384]{0:T(512)S(1)}, u32[]{:S(2)}) copy-start(f32[384]{0:T(512)S(1)} %convert_element_type.103) | copy-start | bytes 4612
  10.2 754.0 %copy-start.25 = (pred[1568]{0:T(1024)(128)(4,1)}, pred[1568]{0:T(1024)(128)(4,1)S(1)}, u32[]{:S(2)}) copy-start(pred[1568]{0:T(1024)(128)(4,1)S(1)} %broadcast_in_dim.20) | copy-start | bytes 4708
  149.2 615.0 %copy-start.3 = (bf16[1568,384]{1,0:T(8,128)(2,1)}, bf16[1568,384]{1,0:T(8,128)(2,1)S(1)}, u32[]{:S(2)}) copy-start(bf16[1568,384]{1,0:T(8,128)(2,1)S(1)} %gather_fusion) | copy-start | bytes 3612676
  163.4 281.3 %reduce-scatter.25.cloned.1.call-start = ((), (), s32[]{:S(2)}) async-start(), calls=%async_computation.22 | async-start | bytes 24084480
  264.7 317.2 %all-gather.23.cloned.1.call-start = ((), (), s32[]{:S(2)}) async-start(), calls=%async_computation.20 | async-start | bytes 3686400 | tf_op jit(solution)/shard_map/all_gather | solution.py:44
  544.6 219.6 %reduce-scatter.13.cloned.1.call-start = ((), (), s32[]{:S(2)}) async-start(), calls=%async_computation.9 | async-start | bytes 12042240 | tf_op jit(solution)/shard_map/reduce_scatter | solution.py:48
  599.7 257.9 %all-gather.17.cloned.1.call-start = ((), (), s32[]{:S(2)}) async-start(), calls=%async_computation.14 | async-start | bytes 6021120 | tf_op jit(solution)/shard_map/all_gather | solution.py:52
  627.2 321.9 %all-gather.13.cloned.1.call-start = ((), (), s32[]{:S(2)}) async-start(), calls=%async_computation.10 | async-start | bytes 6021120 | tf_op jit(solution)/shard_map/all_gather | solution.py:40
  627.4 230.2 %copy-start.16 = (bf16[384,768]{1,0:T(8,128)(2,1)S(1)}, bf16[384,768]{1,0:T(8,128)(2,1)}, u32[]{:S(2)}) copy-start(bf16[384,768]{1,0:T(8,128)(2,1)} %param.23) | copy-start | bytes 1769476
  779.7 386.1 %reduce-scatter.19.cloned.1.call-start = ((), (), s32[]{:S(2)}) async-start(), calls=%async_computation.15 | async-start | bytes 28901376 | tf_op jit(solution)/shard_map/reduce_scatter | solution.py:15
  869.1 514.9 %reduce-scatter.15.cloned.1.call-start = ((), (), s32[]{:S(2)}) async-start(), calls=%async_computation.11 | async-start | bytes 28901376 | tf_op jit(solution)/shard_map/reduce_scatter | solution.py:15
  960.6 569.2 %all-gather.19.cloned.1.call-start = ((), (), s32[]{:S(2)}) async-start(), calls=%async_computation.16 | async-start | bytes 14450688 | tf_op jit(solution)/shard_map/all_gather | solution.py:56
  1409.6 241.9 %all-gather.15.cloned.1.call-start = ((), (), s32[]{:S(2)}) async-start(), calls=%async_computation.12 | async-start | bytes 14450688 | tf_op jit(solution)/shard_map/all_gather | solution.py:44
  1420.7 398.2 %reduce-scatter.21.cloned.1.call-start = ((), (), s32[]{:S(2)}) async-start(), calls=%async_computation.17 | async-start | bytes 12042240 | tf_op jit(solution)/shard_map/reduce_scatter | solution.py:60
  1541.4 445.0 %reduce-scatter.17.cloned.1.call-start = ((), (), s32[]{:S(2)}) async-start(), calls=%async_computation.13 | async-start | bytes 12042240 | tf_op jit(solution)/shard_map/reduce_scatter | solution.py:48
  1662.5 156.4 %copy-start.5 = (f32[1568,384]{1,0:T(8,128)S(1)}, f32[1568,384]{1,0:T(8,128)}, u32[]{:S(2)}) copy-start(f32[1568,384]{1,0:T(8,128)} %get-tuple-element.106) | copy-start | bytes 7225348
  1662.5 420.9 %all-gather.21.cloned.1.call-start = ((), (), s32[]{:S(2)}) async-start(), calls=%async_computation.18 | async-start | bytes 6021120 | tf_op jit(solution)/shard_map/all_gather | solution.py:52
  1991.3 176.1 %reduce-scatter.27.cloned.1.call-start = ((), (), s32[]{:S(2)}) async-start(), calls=%async_computation.23 | async-start | bytes 9633792
  2090.4 235.4 %all-gather.25.cloned.1.call-start = ((), (), s32[]{:S(2)}) async-start(), calls=%async_computation.21 | async-start | bytes 11059200 | tf_op jit(solution)/shard_map/all_gather | solution.py:56
  2233.0 228.9 %all-reduce.9.cloned.1.call-start = ((), (), s32[]{:S(2)}) async-start(), calls=%async_computation.24 | async-start | bytes 7077888 | tf_op jit(solution)/shard_map/psum | solution.py:224
  2386.4 243.0 %reduce-scatter.23.cloned.1.call-start = ((), (), s32[]{:S(2)}) async-start(), calls=%async_computation.19 | async-start | bytes 12042240 | tf_op jit(solution)/shard_map/reduce_scatter | solution.py:60
  2419.3 210.1 %copy-start.4 = (bf16[1568,384]{1,0:T(8,128)(2,1)S(1)}, bf16[1568,384]{1,0:T(8,128)(2,1)}, u32[]{:S(2)}) copy-start(bf16[1568,384]{1,0:T(8,128)(2,1)} %copy-done.3) | copy-start | bytes 3612676
  2419.3 210.1 %copy-start.22 = (f32[1568]{0:T(1024)S(1)}, f32[1568]{0:T(1024)}, u32[]{:S(2)}) copy-start(f32[1568]{0:T(1024)} %copy-done.21) | copy-start | bytes 18820
  2419.3 210.1 %copy-start.24 = (f32[1568]{0:T(1024)S(1)}, f32[1568]{0:T(1024)}, u32[]{:S(2)}) copy-start(f32[1568]{0:T(1024)} %copy-done.23) | copy-start | bytes 18820
  2419.3 210.1 %copy-start.26 = (pred[1568]{0:T(1024)(128)(4,1)S(1)}, pred[1568]{0:T(1024)(128)(4,1)}, u32[]{:S(2)}) copy-start(pred[1568]{0:T(1024)(128)(4,1)} %copy-done.25) | copy-start | bytes 4708
  2419.4 210.1 %copy-start.28 = (f32[384]{0:T(512)S(1)}, f32[384]{0:T(512)}, u32[]{:S(2)}) copy-start(f32[384]{0:T(512)} %copy-done.27) | copy-start | bytes 4612
  2671.8 51.4 %copy-start.15 = (f32[384,3,192]{0,2,1:T(8,128)S(1)}, f32[384,3,192]{0,2,1:T(8,128)}, u32[]{:S(2)}) copy-start(f32[384,3,192]{0,2,1:T(8,128)} %get-tuple-element.127) | copy-start | bytes 2654212
  2671.8 52.3 %copy-start.19 = (f32[192,384]{1,0:T(8,128)S(1)}, f32[192,384]{1,0:T(8,128)}, u32[]{:S(2)}) copy-start(f32[192,384]{1,0:T(8,128)} %get-tuple-element.129) | copy-start | bytes 884740
  2671.8 53.0 %copy-start.14 = (f32[384,768]{1,0:T(8,128)S(1)}, f32[384,768]{1,0:T(8,128)}, u32[]{:S(2)}) copy-start(f32[384,768]{1,0:T(8,128)} %get-tuple-element.131) | copy-start | bytes 3538948
  2671.8 54.0 %copy-start.1 = (bf16[384,768]{1,0:T(8,128)(2,1)S(1)}, bf16[384,768]{1,0:T(8,128)(2,1)}, u32[]{:S(2)}) copy-start(bf16[384,768]{1,0:T(8,128)(2,1)} %param.21) | copy-start | bytes 1769476
  (30 other events, 319.0 us)
Sparse Core Ops, SparseCore 0:
  163.5 91.2 all-gather.10
  264.9 179.8 reduce-scatter.24
  544.7 37.1 all-gather.22
  599.8 164.3 reduce-scatter.12
  765.6 91.9 all-gather.16
  859.6 89.4 all-gather.12
  951.4 214.3 reduce-scatter.18
  1168.1 215.8 reduce-scatter.14
  1409.7 120.1 all-gather.18
  1531.3 120.1 all-gather.14
  1654.4 164.3 reduce-scatter.20
  1821.1 165.2 reduce-scatter.16
  1991.4 91.9 all-gather.20
  2090.5 76.8 reduce-scatter.26
  2233.2 92.5 all-gather.24
  2386.6 75.3 all-reduce.8
  2464.9 164.4 reduce-scatter.22
where the time goes:
time: 2740 us; the launch traced here: 2730 us
  waiting for transfers between devices  1990 us (73%)
  local copies, waits for them, and re-layouts  283 us (10%)
  other arithmetic  233 us (9%)
  matrix products  134 us (5%)
  blocking collectives  78.4 us (3%)
    reduce_scatter x2, waiting for transfers between devices, narrow_product(): lax.psum_scatter(jnp.dot(acts, weight, preferred_element_type=jnp.float32...  423 us
    reduce_scatter x2, waiting for transfers between devices, grad_wide_sum(): lax.psum_scatter(partial_rows, 'wide', scatter_dimension=0, tiled=True)  320 us
    reduce_scatter x2, waiting for transfers between devices, wide_sum(): lax.psum_scatter(partial_rows, 'wide', scatter_dimension=0, tiled=True)  294 us
    unnamed x19, waiting for transfers between devices  256 us
    all_gather x2, waiting for transfers between devices, grad_narrow_rows(): return lax.all_gather(acts, 'narrow', axis=0, tiled=True)  177 us
    all_gather x2, waiting for transfers between devices, wide_rows(): return lax.all_gather(acts, 'wide', axis=0, tiled=True)  171 us
    all_gather x2, waiting for transfers between devices, grad_wide_rows(): return lax.all_gather(acts, 'wide', axis=0, tiled=True)  170 us
    unnamed x10, other arithmetic  148 us
  transfers between devices with their start and end apart: 17, of which 17 were waited for; matrix products, arithmetic and copies ran while one was open for 6% of the time, Pallas kernels for 0%

commit v1 on v0

--- a/solution.py
+++ b/solution.py
@@ -1,3 +1,4 @@
+import functools
 from functools import partial
 import jax
 import jax.numpy as jnp
@@ -9,6 +10,34 @@
 PATCHES = 196
 VISIBLE = 49
 epsilon = 1e-06
+
+
+def resolve_spot(xx, in_dim):
+    xx = jnp.moveaxis(xx, 0, in_dim)
+    f_next = xx.shape
+    return xx.reshape(*f_next[:in_dim], f_next[in_dim] * f_next[in_dim + 1], *f_next[in_dim + 2 :])
+
+
+def vector_order(mine, named_axis):
+    everything = mine[None]
+    nd = lax.psum(1, named_axis)
+    for m in range(nd.bit_length() - 1):
+        taken_in = 1 << m
+        upper = lax.ppermute(
+            everything, named_axis, [(hop_no, hop_no ^ taken_in) for hop_no in range(nd)]
+        )
+        t1 = jnp.stack([everything, upper], axis=0)
+        vec_out = lax.axis_index(named_axis) >> m & 1
+        everything = jnp.where(vec_out == 0, t1, t1[::-1]).reshape(-1, *mine.shape)
+    return everything
+
+
+def save_edge(u, tile_in, which_dim):
+    ready = vector_order(u, tile_in)
+    return resolve_spot(ready, which_dim)
+
+
+switch_target = functools.partial(save_edge, tile_in="narrow", which_dim=0)
 
 
 def narrow_product(acts, weight):
@@ -41,7 +70,7 @@
 
 
 def narrow_rows(acts):
-    return lax.all_gather(acts, "narrow", axis=0, tiled=True)
+    return switch_target(acts)
 
 
 def wide_sum(partial_rows):

time: 2740 us -> 2620 us (0.956)
  waiting for transfers between devices: 1990 us -> 1830 us
  other arithmetic: 233 us -> 266 us
    all_gather x2 -> x0, waiting for transfers between devices: 147 us -> none  [narrow_rows(): return lax.all_gather(acts, 'narrow', axis=0, tiled=True)]
    reduce_scatter x2, waiting for transfers between devices: 320 us -> 180 us  [grad_wide_sum(): lax.psum_scatter(partial_rows, 'wide', scatter_dimension=0, tiled=True)]
    ppermute x0 -> x2, waiting for transfers between devices: none -> 119 us  [vector_order(): lax.ppermute(everything, named_axis, [(hop_no, hop_no ^ taken_in) for hop...]
    unnamed x105 -> x103, local copies, waits for them, and re-layouts: 97.1 us -> 78 us
    unnamed x19 -> x17, waiting for transfers between devices: 256 us -> 256 us
  transfers between devices with their start and end apart: 17 -> 17, of which waited for: 17 -> 17; matrix products, arithmetic and copies ran while one was open for 6% -> 7% of each run, Pallas kernels for 0% -> 0%
where the time goes in v1:
time: 2620 us; the launch traced here: 2600 us
  waiting for transfers between devices  1830 us (70%)
  local copies, waits for them, and re-layouts  279 us (11%)
  other arithmetic  266 us (10%)
  matrix products  134 us (5%)
  blocking collectives  78 us (3%)
    reduce_scatter x2, waiting for transfers between devices, narrow_product(): lax.psum_scatter(jnp.dot(acts, weight, preferred_element_type=jnp.float32...  423 us
    reduce_scatter x2, waiting for transfers between devices, wide_sum(): lax.psum_scatter(partial_rows, 'wide', scatter_dimension=0, tiled=True)  294 us
    unnamed x17, waiting for transfers between devices  256 us
    all_gather x2, waiting for transfers between devices, grad_narrow_rows(): return lax.all_gather(acts, 'narrow', axis=0, tiled=True)  188 us
    reduce_scatter x2, waiting for transfers between devices, grad_wide_sum(): lax.psum_scatter(partial_rows, 'wide', scatter_dimension=0, tiled=True)  180 us
    all_gather x2, waiting for transfers between devices, wide_rows(): return lax.all_gather(acts, 'wide', axis=0, tiled=True)  171 us
    all_gather x2, waiting for transfers between devices, grad_wide_rows(): return lax.all_gather(acts, 'wide', axis=0, tiled=True)  170 us
    unnamed x10, other arithmetic  148 us
  transfers between devices with their start and end apart: 17, of which 17 were waited for; matrix products, arithmetic and copies ran while one was open for 7% of the time, Pallas kernels for 0%

profile of v1, /device:TPU:0, one launch (start us, length us, event | category | flops | bytes accessed | tf_op | source)
XLA Modules:
  0.0 2604.3 jit_solution(17130178608924197324)
XLA Ops:
  10.3 103.4 %reduce.4 = bf16[2408448]{0:T(1024)(128)(2,1)} reduce(bf16[1,2408448]{1,0:T(2,128)(2,1)} %param.15, bf16[]{:T(256)} %constant.132), dimensions={0}, to_apply=%param.15.reduce_sub_computation | reduce | bytes 9633794 | tf_op args[0]
  126.9 22.3 gather_fusion
  163.6 91.2 %all-gather.8.cloned.1.call-done = bf16[6272,384]{1,0:T(8,128)(2,1)} async-done(((bf16[1568,384]{1,0:T(8,128)(2,1)}), bf16[6272,384]{1,0:T(8,128)(2,1)}) %all-gather.8.cloned.1.call-update) | async-done | bytes 4816912 | tf_op jit(solution)/shard_map/all_gather | solution.py:69
  265.4 179.2 %reduce-scatter.25.cloned.1.call-done = f32[3136,576]{1,0:T(8,128)} async-done(((f32[6272,576]{1,0:T(8,128)}), f32[3136,576]{1,0:T(8,128)}) %reduce-scatter.25.cloned.1.call-update) | async-done | bytes 7225360
  459.2 29.2 %reshape.146 = bf16[64,49,3,3,64]{1,0,4,3,2:T(8,128)(2,1)} reshape(bf16[3136,576]{0,1:T(8,128)(2,1)} %add_convert_fusion.1) | data formatting | bytes 7225344 | tf_op jit(solution)/shard_map/reshape | solution.py:193
  541.8 23.6 collective-permute-done
  583.5 26.2 %reduce.5 = bf16[602112]{0:T(1024)(128)(2,1)S(1)} reduce(bf16[1,602112]{1,0:T(2,128)(2,1)} %param.29, bf16[]{:T(256)} %constant.132), dimensions={0}, to_apply=%param.29.reduce_sub_computation | reduce | bytes 2408450 | tf_op args[14]
  611.3 136.7 %reduce-scatter.13.cloned.1.call-done = f32[1568,384]{1,0:T(8,128)} async-done(((f32[6272,384]{1,0:T(8,128)}), f32[1568,384]{1,0:T(8,128)}) %reduce-scatter.13.cloned.1.call-update) | async-done | bytes 2408464 | tf_op jit(solution)/shard_map/reduce_scatter | solution.py:77
  763.2 78.2 %all-gather.12.cloned.1.call-done = bf16[6272,384]{1,0:T(8,128)(2,1)} async-done(((bf16[1568,384]{1,0:T(8,128)(2,1)}), bf16[6272,384]{1,0:T(8,128)(2,1)}) %all-gather.12.cloned.1.call-update) | async-done | bytes 4816912 | tf_op jit(solution)/shard_map/all_gather | solution.py:81
  853.0 79.8 %all-gather.10.cloned.1.call-done = bf16[6272,384]{1,0:T(8,128)(2,1)} async-done(((bf16[1568,384]{1,0:T(8,128)(2,1)}), bf16[6272,384]{1,0:T(8,128)(2,1)}) %all-gather.10.cloned.1.call-update) | async-done | bytes 4816912 | tf_op jit(solution)/shard_map/all_gather | solution.py:69
  945.1 204.3 %reduce-scatter.19.cloned.1.call-done = f32[3136,768]{1,0:T(8,128)} async-done(((f32[6272,768]{1,0:T(8,128)}), f32[3136,768]{1,0:T(8,128)}) %reduce-scatter.19.cloned.1.call-update) | async-done | bytes 9633808 | tf_op jit(solution)/shard_map/reduce_scatter | solution.py:44
  1149.4 218.2 %reduce-scatter.15.cloned.1.call-done = f32[3136,768]{1,0:T(8,128)} async-done(((f32[6272,768]{1,0:T(8,128)}), f32[3136,768]{1,0:T(8,128)}) %reduce-scatter.15.cloned.1.call-update) | async-done | bytes 9633808 | tf_op jit(solution)/shard_map/reduce_scatter | solution.py:44
  1367.6 25.8 add_convert_fusion
  1393.5 120.3 %all-gather.14.cloned.1.call-done = bf16[6272,768]{1,0:T(8,128)(2,1)} async-done(((bf16[3136,768]{1,0:T(8,128)(2,1)}), bf16[6272,768]{1,0:T(8,128)(2,1)}) %all-gather.14.cloned.1.call-update) | async-done | bytes 9633808 | tf_op jit(solution)/shard_map/all_gather | solution.py:85
  1545.6 95.5 %collective-permute-done.1 = bf16[1,3136,768]{2,1,0:T(8,128)(2,1)} collective-permute-done((bf16[1,3136,768]{2,1,0:T(8,128)(2,1)}, bf16[1,3136,768]{2,1,0:T(8,128)(2,1)}, u32[]{:S(2)}, u32[]{:S(2)}) %collective-permute-start.1) | collective-permute-done | bytes 4816928 | tf_op jit(solution)/shard_map/ppermute | solution.py:26
  1649.7 12.4 reverse_select_fusion
  1674.1 15.4 reduce-scatter.21.cloned.1.call-done
  1700.4 157.2 %reduce-scatter.17.cloned.1.call-done = f32[1568,384]{1,0:T(8,128)} async-done(((f32[6272,384]{1,0:T(8,128)}), f32[1568,384]{1,0:T(8,128)}) %reduce-scatter.17.cloned.1.call-update) | async-done | bytes 2408464 | tf_op jit(solution)/shard_map/reduce_scatter | solution.py:77
  1862.5 92.0 %all-gather.16.cloned.1.call-done = bf16[6272,384]{1,0:T(8,128)(2,1)} async-done(((bf16[1568,384]{1,0:T(8,128)(2,1)}), bf16[6272,384]{1,0:T(8,128)(2,1)}) %all-gather.16.cloned.1.call-update) | async-done | bytes 4816912 | tf_op jit(solution)/shard_map/all_gather | solution.py:81
  1961.7 77.0 %reduce-scatter.27.cloned.1.call-done = f32[3136,192]{1,0:T(8,128)} async-done(((f32[6272,192]{1,0:T(8,128)}), f32[3136,192]{1,0:T(8,128)}) %reduce-scatter.27.cloned.1.call-update) | async-done | bytes 2408464
  2075.9 13.5 copy.76
  2089.4 15.0 reshape.173
  2129.0 68.2 %all-gather.18.cloned.1.call-done = bf16[2,3136,576]{1,2,0:T(8,128)(2,1)} async-done(((bf16[1,3136,576]{1,2,0:T(8,128)(2,1)}), bf16[2,3136,576]{1,2,0:T(8,128)(2,1)}) %all-gather.18.cloned.1.call-update) | async-done | bytes 7225360 | tf_op jit(solution)/shard_map/all_gather | solution.py:85
  2197.2 39.5 %copy.77 = bf16[2,3136,576]{1,0,2:T(2,128)(2,1)} copy(bf16[2,3136,576]{1,2,0:T(8,128)(2,1)} %all-gather.18.cloned.1.call-done) | data formatting | bytes 14450688 | tf_op jit(solution)/shard_map/all_gather | solution.py:85
  2236.7 11.8 reshape.174
  2291.9 11.7 all-reduce.1
  2303.6 29.8 %all-reduce.9.cloned.1.call-done = (f32[384,3,192]{0,2,1:T(8,128)}, f32[192,384]{1,0:T(8,128)}, f32[384,768]{1,0:T(8,128)}, f32[384,768]{0,1:T(8,128)}) async-done(((f32[384,3,192]{0,2,1:T(8,128)}, f32[192,384]{1,0:T(8,128)}, f32[384,768]{1,0:T(8,128)}, f32[384,768]{0,1:T(8,128)}), (f32[384,3,192]{0,2,1:T(8,128)}, f32[192,384]{1,0:T(8,128)}, f32[384,768]{1,0:T(8,128)}, ...) | async-done | bytes 3538960 | tf_op jit(solution)/shard_map/psum | solution.py:253
  2336.1 164.8 %reduce-scatter.23.cloned.1.call-done = f32[1568,384]{1,0:T(8,128)} async-done(((f32[6272,384]{1,0:T(8,128)}), f32[1568,384]{1,0:T(8,128)}) %reduce-scatter.23.cloned.1.call-update) | async-done | bytes 2408464 | tf_op jit(solution)/shard_map/reduce_scatter | solution.py:89
  2512.0 18.2 scatter_custom_fusion
  2530.2 13.1 copy.78
  2543.3 18.9 reshape.151
  2562.1 32.5 %all-reduce = (f32[384]{0:T(512)}, f32[384]{0:T(512)}, f32[384]{0:T(512)}, f32[384]{0:T(512)}) all-reduce(f32[384]{0:T(512)S(1)} %get-tuple-element.72, f32[384]{0:T(512)S(1)} %get-tuple-element.77, f32[384]{0:T(512)S(1)} %get-tuple-element.70, f32[384]{0:T(512)S(1)} %get-tuple-element.76), channel_id=1, replica_groups=mesh['dp'=4,'wide'=4,'narrow'=2] {'dp','wide'}, use_global_device_ids=true, to_apply=%region_41.42 | all-reduce | flops 1536 | bytes 12288 | tf_op jit(solution)/shard_map/psum | solution.py:254
  (220 shorter events, 364.3 us)
Async XLA Ops:
  7.2 925.7 %copy-start = (bf16[384,768]{1,0:T(8,128)(2,1)S(1)}, bf16[384,768]{1,0:T(8,128)(2,1)}, u32[]{:S(2)}) copy-start(bf16[384,768]{1,0:T(8,128)(2,1)} %param.21) | copy-start | bytes 1769476
  7.2 247.6 %all-gather.8.cloned.1.call-start = ((), (), s32[]{:S(2)}) async-start(), calls=%async_computation.8 | async-start | bytes 6021120 | tf_op jit(solution)/shard_map/all_gather | solution.py:69
  9.4 151.2 %copy-start.27 = (f32[384]{0:T(512)}, f32[384]{0:T(512)S(1)}, u32[]{:S(2)}) copy-start(f32[384]{0:T(512)S(1)} %convert_element_type.121) | copy-start | bytes 4612
  10.2 737.8 %copy-start.25 = (pred[1568]{0:T(1024)(128)(4,1)}, pred[1568]{0:T(1024)(128)(4,1)S(1)}, u32[]{:S(2)}) copy-start(pred[1568]{0:T(1024)(128)(4,1)S(1)} %broadcast_in_dim.22) | copy-start | bytes 4708
  149.1 598.8 %copy-start.3 = (bf16[1568,384]{1,0:T(8,128)(2,1)}, bf16[1568,384]{1,0:T(8,128)(2,1)S(1)}, u32[]{:S(2)}) copy-start(bf16[1568,384]{1,0:T(8,128)(2,1)S(1)} %gather_fusion) | copy-start | bytes 3612676
  163.3 281.4 %reduce-scatter.25.cloned.1.call-start = ((), (), s32[]{:S(2)}) async-start(), calls=%async_computation.20 | async-start | bytes 24084480
  264.7 483.3 %reduce-scatter.13.cloned.1.call-start = ((), (), s32[]{:S(2)}) async-start(), calls=%async_computation.9 | async-start | bytes 12042240 | tf_op jit(solution)/shard_map/reduce_scatter | solution.py:77
  536.3 29.1 %collective-permute-start = (bf16[1,3136,192]{1,2,0:T(8,128)(2,1)}, bf16[1,3136,192]{1,2,0:T(8,128)(2,1)}, u32[]{:S(2)}, u32[]{:S(2)}) collective-permute-start(bf16[1,3136,192]{1,2,0:T(8,128)(2,1)} %convert_element_type.133), channel_id=1, source_target_pairs={{0,1},{1,0},{2,3},{3,2},{4,5},{5,4},{6,7},{7,6},{8,9},{9,8},{10,11... | collective-permute-start | bytes 3612680 | tf_op jit(solution)/shard_map/ppermute | solution.py:26
  583.4 27.8 %copy-start.33 = (bf16[384]{0:T(512)(128)(2,1)S(1)}, bf16[384]{0:T(512)(128)(2,1)}, u32[]{:S(2)}) copy-start(bf16[384]{0:T(512)(128)(2,1)} %param.28) | copy-start | bytes 2308
  583.5 257.9 %all-gather.12.cloned.1.call-start = ((), (), s32[]{:S(2)}) async-start(), calls=%async_computation.13 | async-start | bytes 6021120 | tf_op jit(solution)/shard_map/all_gather | solution.py:81
  611.1 321.7 %all-gather.10.cloned.1.call-start = ((), (), s32[]{:S(2)}) async-start(), calls=%async_computation.10 | async-start | bytes 6021120 | tf_op jit(solution)/shard_map/all_gather | solution.py:69
  611.3 230.1 %copy-start.16 = (bf16[384,768]{1,0:T(8,128)(2,1)S(1)}, bf16[384,768]{1,0:T(8,128)(2,1)}, u32[]{:S(2)}) copy-start(bf16[384,768]{1,0:T(8,128)(2,1)} %param.23) | copy-start | bytes 1769476
  763.1 386.3 %reduce-scatter.19.cloned.1.call-start = ((), (), s32[]{:S(2)}) async-start(), calls=%async_computation.14 | async-start | bytes 28901376 | tf_op jit(solution)/shard_map/reduce_scatter | solution.py:44
  853.0 514.7 %reduce-scatter.15.cloned.1.call-start = ((), (), s32[]{:S(2)}) async-start(), calls=%async_computation.11 | async-start | bytes 28901376 | tf_op jit(solution)/shard_map/reduce_scatter | solution.py:44
  944.4 569.3 %all-gather.14.cloned.1.call-start = ((), (), s32[]{:S(2)}) async-start(), calls=%async_computation.15 | async-start | bytes 14450688 | tf_op jit(solution)/shard_map/all_gather | solution.py:85
  1393.5 296.1 %reduce-scatter.21.cloned.1.call-start = ((), (), s32[]{:S(2)}) async-start(), calls=%async_computation.16 | async-start | bytes 12042240 | tf_op jit(solution)/shard_map/reduce_scatter | solution.py:89
  1525.0 332.7 %reduce-scatter.17.cloned.1.call-start = ((), (), s32[]{:S(2)}) async-start(), calls=%async_computation.12 | async-start | bytes 12042240 | tf_op jit(solution)/shard_map/reduce_scatter | solution.py:77
  1535.5 105.6 %collective-permute-start.1 = (bf16[1,3136,768]{2,1,0:T(8,128)(2,1)}, bf16[1,3136,768]{2,1,0:T(8,128)(2,1)}, u32[]{:S(2)}, u32[]{:S(2)}) collective-permute-start(bf16[1,3136,768]{2,1,0:T(8,128)(2,1)} %fusion.107), channel_id=1, source_target_pairs={{0,1},{1,0},{2,3},{3,2},{4,5},{5,4},{6,7},{7,6},{8,9},{9,8},{10,11... | collective-permute-start | bytes 14450696 | tf_op jit(solution)/shard_map/ppermute | solution.py:26
  1673.4 281.1 %all-gather.16.cloned.1.call-start = ((), (), s32[]{:S(2)}) async-start(), calls=%async_computation.17 | async-start | bytes 6021120 | tf_op jit(solution)/shard_map/all_gather | solution.py:81
  1862.5 176.1 %reduce-scatter.27.cloned.1.call-start = ((), (), s32[]{:S(2)}) async-start(), calls=%async_computation.21 | async-start | bytes 9633792
  1961.6 235.6 %all-gather.18.cloned.1.call-start = ((), (), s32[]{:S(2)}) async-start(), calls=%async_computation.19 | async-start | bytes 11059200 | tf_op jit(solution)/shard_map/all_gather | solution.py:85
  2104.5 229.0 %all-reduce.9.cloned.1.call-start = ((), (), s32[]{:S(2)}) async-start(), calls=%async_computation.22 | async-start | bytes 7077888 | tf_op jit(solution)/shard_map/psum | solution.py:253
  2257.9 243.0 %reduce-scatter.23.cloned.1.call-start = ((), (), s32[]{:S(2)}) async-start(), calls=%async_computation.18 | async-start | bytes 12042240 | tf_op jit(solution)/shard_map/reduce_scatter | solution.py:89
  2290.7 210.1 %copy-start.4 = (bf16[1568,384]{1,0:T(8,128)(2,1)S(1)}, bf16[1568,384]{1,0:T(8,128)(2,1)}, u32[]{:S(2)}) copy-start(bf16[1568,384]{1,0:T(8,128)(2,1)} %copy-done.3) | copy-start | bytes 3612676
  2290.7 210.1 %copy-start.22 = (f32[1568]{0:T(1024)S(1)}, f32[1568]{0:T(1024)}, u32[]{:S(2)}) copy-start(f32[1568]{0:T(1024)} %copy-done.21) | copy-start | bytes 18820
  2290.8 210.1 %copy-start.24 = (f32[1568]{0:T(1024)S(1)}, f32[1568]{0:T(1024)}, u32[]{:S(2)}) copy-start(f32[1568]{0:T(1024)} %copy-done.23) | copy-start | bytes 18820
  2290.8 210.1 %copy-start.26 = (pred[1568]{0:T(1024)(128)(4,1)S(1)}, pred[1568]{0:T(1024)(128)(4,1)}, u32[]{:S(2)}) copy-start(pred[1568]{0:T(1024)(128)(4,1)} %copy-done.25) | copy-start | bytes 4708
  2290.8 210.1 %copy-start.28 = (f32[384]{0:T(512)S(1)}, f32[384]{0:T(512)}, u32[]{:S(2)}) copy-start(f32[384]{0:T(512)} %copy-done.27) | copy-start | bytes 4612
  2543.3 51.4 %copy-start.15 = (f32[384,3,192]{0,2,1:T(8,128)S(1)}, f32[384,3,192]{0,2,1:T(8,128)}, u32[]{:S(2)}) copy-start(f32[384,3,192]{0,2,1:T(8,128)} %get-tuple-element.127) | copy-start | bytes 2654212
  2543.3 52.3 %copy-start.19 = (f32[192,384]{1,0:T(8,128)S(1)}, f32[192,384]{1,0:T(8,128)}, u32[]{:S(2)}) copy-start(f32[192,384]{1,0:T(8,128)} %get-tuple-element.129) | copy-start | bytes 884740
  2543.3 53.0 %copy-start.14 = (f32[384,768]{1,0:T(8,128)S(1)}, f32[384,768]{1,0:T(8,128)}, u32[]{:S(2)}) copy-start(f32[384,768]{1,0:T(8,128)} %get-tuple-element.131) | copy-start | bytes 3538948
  2543.3 54.0 %copy-start.1 = (bf16[384,768]{1,0:T(8,128)(2,1)S(1)}, bf16[384,768]{1,0:T(8,128)(2,1)}, u32[]{:S(2)}) copy-start(bf16[384,768]{1,0:T(8,128)(2,1)} %param.21) | copy-start | bytes 1769476
  (30 other events, 268.8 us)
Sparse Core Ops, SparseCore 0:
  163.4 91.3 all-gather.7
  264.8 179.8 reduce-scatter.24
  583.5 164.3 reduce-scatter.12
  749.4 91.9 all-gather.11
  843.4 89.4 all-gather.9
  935.0 214.3 reduce-scatter.18
  1151.7 215.8 reduce-scatter.14
  1393.6 120.1 all-gather.13
  1525.1 164.3 reduce-scatter.20
  1692.3 165.2 reduce-scatter.16
  1862.6 91.9 all-gather.15
  1961.7 76.8 reduce-scatter.26
  2104.6 92.5 all-gather.17
  2258.0 75.3 all-reduce.8
  2336.3 164.4 reduce-scatter.22
